TPU v7x, 256 devices: a whole 4x4x8 slice. The times are simulated.
256 devices in a mesh: space: 16 (over z, y_lo), snap: 16 (over y_hi, x, core).
Axes of the slice: x: 4, y: 4 (y_hi: 2, y_lo: 2; y = y_hi * 2 + y_lo), z: 8, core: 2. Of those that a mesh axis runs over, the one named last changes fastest.
Arguments:
- primal: bfloat16 [2048, 196608], P('snap', 'space'), may hold values from -6 to 6
- adjoint_pencils: bfloat16 [1024, 196608], P('snap', 'space'), may hold values from -0.01953125 to 0.01953125
- weights: float32 [196608], P('space'), may hold values from 0.2 to 2
- pencil_map: int32 [1536], replicated, may hold values from 0 to 1535, as said below
Outputs:
- hankel: float32 [1024, 2048], P('space', 'snap')
Inputs may be any that keep to these rules, and one draw needn't show every extreme that they name: `pencil_map`: each number appears once; each aligned block of 96 entries holds exactly 6 entries from every aligned range of 96 values.
All inputs are finite; a program needn't handle non-finite values.
Results may differ from a plain program's by a relative error of at most 0.0029.
Values may be sent and summed in bfloat16 or wider, within the bound.
A program may use at most 128 MiB of HBM per device.

v0:
```python
import jax
import jax.numpy as jnp
from jax import lax
from jax.sharding import PartitionSpec as P

PEN_LEN = 128


def on_device(primal, adjoint_pencils, weights, pencil_map):
    rows_here = adjoint_pencils.shape[0]
    points = adjoint_pencils.shape[1]
    pen_dev = points // PEN_LEN
    tiles = lax.axis_size("space")
    share = pen_dev // tiles
    place = lax.axis_index("space")
    weighted = (primal.astype(jnp.float32) * weights[None, :]).astype(jnp.bfloat16)
    all_slots = pencil_map.reshape(tiles, pen_dev)
    targets = all_slots // pen_dev
    orders = jnp.argsort(targets, axis=1, stable=True)
    own_order = lax.dynamic_index_in_dim(orders, place, 0, keepdims=False)
    chosen = lax.dynamic_slice_in_dim(orders, place * share, share, 1)
    arrived = (jnp.take_along_axis(all_slots, chosen, axis=1) - place * pen_dev).reshape(pen_dev)
    blocks = adjoint_pencils.reshape(rows_here, pen_dev, PEN_LEN)
    outgoing = jnp.take(blocks, own_order, axis=1).reshape(rows_here, tiles, share, PEN_LEN)
    incoming = lax.all_to_all(outgoing, "space", split_axis=1, concat_axis=1, tiled=True)
    inverse = jnp.argsort(arrived)
    moving = jnp.take(incoming.reshape(rows_here, pen_dev, PEN_LEN), inverse, axis=1).reshape(
        rows_here, points
    )
    product = lax.dot_general(
        lax.all_gather(moving, "snap", axis=0, tiled=True),
        weighted,
        (((1,), (1,)), ((), ())),
        preferred_element_type=jnp.float32,
    )
    return lax.psum_scatter(product, "space", scatter_dimension=0, tiled=True)


def solution(mesh):
    placed = (P("snap", "space"), P("snap", "space"), P("space"), P())
    return jax.shard_map(
        on_device, mesh=mesh, in_specs=placed, out_specs=P("space", "snap"), check_vma=False
    )
```

profile of v0, /device:TPU:4, one launch (start us, length us, event | category | flops | bytes accessed | tf_op | source)
XLA Modules:
  0.0 308.7 jit_solution(8084344282338904994)
XLA Ops:
  6.5 0.9 reshape.38
  7.4 0.1 copy.12
  7.5 1.5 sort.34
  9.1 0.2 dynamic-slice_reduce_fusion
  9.3 0.4 copy_bitcast_fusion.1
  9.7 2.0 gather_fusion.1
  11.7 2.8 broadcast_select_fusion
  14.5 9.6 %all-to-all-start = ((bf16[64,16,6,128]{3,0,2,1:T(8,128)(2,1)}), bf16[64,16,6,128]{3,0,2,1:T(8,128)(2,1)S(1)}, u32[]{:S(2)}, u32[]{:S(2)}) async-start(bf16[64,16,6,128]{3,0,2,1:T(8,128)(2,1)} %bitcast.21), calls=%async_computation | async-start | bytes 3145728 | tf_op jit(solution)/shard_map/all_to_all | solution.py:25
  24.1 0.0 all-gather.2.cloned.1.call-start
  24.1 0.1 copy.13
  24.2 0.1 reshape.59
  24.3 1.2 gather_fusion
  25.6 0.1 reshape.62
  25.6 0.1 copy.14
  25.7 0.1 copy.15
  25.8 0.1 sub.19
  25.9 2.5 sort.35
  28.5 35.2 %all-to-all-done = bf16[64,16,6,128]{3,0,2,1:T(8,128)(2,1)S(1)} async-done(((bf16[64,16,6,128]{3,0,2,1:T(8,128)(2,1)}), bf16[64,16,6,128]{3,0,2,1:T(8,128)(2,1)S(1)}, u32[]{:S(2)}, u32[]{:S(2)}) %all-to-all-start) | async-done | bytes 1572896 | tf_op jit(solution)/shard_map/all_to_all | solution.py:25
  63.7 2.0 gather_fusion.2
  65.6 3.0 copy_bitcast_fusion
  68.6 0.0 reduce-scatter.2.cloned.1.call-start
  68.7 149.1 %all-gather.2.cloned.1.call-done = bf16[1024,12288]{1,0:T(8,128)(2,1)} async-done(((bf16[64,12288]{1,0:T(8,128)(2,1)}), bf16[1024,12288]{1,0:T(8,128)(2,1)}) %all-gather.2.cloned.1.call-update) | async-done | bytes 25165840 | tf_op jit(solution)/shard_map/all_gather | solution.py:31
  217.8 13.2 %fusion = f32[1024,128]{1,0:T(8,128)} fusion(bf16[1024,12288]{1,0:T(8,128)(2,1)} %all-gather.2.cloned.1.call-done, bf16[128,12288]{1,0:T(8,128)(2,1)} %param.6, f32[12288]{0:T(1024)S(1)} %copy-done.1), kind=kOutput, calls=%fused_computation.4 | convolution fusion | flops 3225944064 | bytes 28884992 | tf_op jit(solution)/shard_map/dot_general | solution.py:30
  231.0 70.9 %reduce-scatter.2.cloned.1.call-done = f32[64,128]{1,0:T(8,128)} async-done(((f32[1024,128]{1,0:T(8,128)}), f32[64,128]{1,0:T(8,128)}) %reduce-scatter.2.cloned.1.call-update) | async-done | bytes 32784 | tf_op jit(solution)/shard_map/reduce_scatter | solution.py:36
  (17 shorter events, 0.1 us)
Async XLA Ops:
  6.5 2.7 copy-start
  14.5 49.2 %all-to-all-start = ((bf16[64,16,6,128]{3,0,2,1:T(8,128)(2,1)}), bf16[64,16,6,128]{3,0,2,1:T(8,128)(2,1)S(1)}, u32[]{:S(2)}, u32[]{:S(2)}) async-start(bf16[64,16,6,128]{3,0,2,1:T(8,128)(2,1)} %bitcast.21), calls=%async_computation | async-start | bytes 3145728 | tf_op jit(solution)/shard_map/all_to_all | solution.py:25
  24.1 193.7 %all-gather.2.cloned.1.call-start = ((), (), s32[]{:S(2)}) async-start(), calls=%async_computation.2 | async-start | bytes 26738688 | tf_op jit(solution)/shard_map/all_gather | solution.py:31
  68.6 149.2 %copy-start.1 = (f32[12288]{0:T(1024)S(1)}, f32[12288]{0:T(1024)}, u32[]{:S(2)}) copy-start(f32[12288]{0:T(1024)} %param.8) | copy-start | bytes 147460
  68.6 233.3 %reduce-scatter.2.cloned.1.call-start = ((), (), s32[]{:S(2)}) async-start(), calls=%async_computation.3 | async-start | bytes 557056 | tf_op jit(solution)/shard_map/reduce_scatter | solution.py:36
Sparse Core Ops, SparseCore 0:
  68.8 149.0 all-gather.1
  231.1 70.7 reduce-scatter.1
where the time goes:
time: 309 us
  waiting for transfers between devices  255 us (83%)
  between operations  13.5 us (4%)
  matrix products  13.2 us (4%)
  other arithmetic  9.89 us (3%)
  starting transfers between devices  9.67 us (3%)
  local copies, waits for them, and re-layouts  7.27 us (2%)
    all_gather x1, waiting for transfers between devices, on_device(): lax.all_gather(moving, 'snap', axis=0, tiled=True)  149 us
    reduce_scatter x1, waiting for transfers between devices, on_device(): return lax.psum_scatter(product, 'space', scatter_dimension=0, tiled=True)  70.9 us
    all_to_all x1, waiting for transfers between devices, on_device(): lax.all_to_all(outgoing, 'space', split_axis=1, concat_axis=1, tiled=True)  35.2 us
    dot_general x1, matrix products, on_device(): lax.dot_general(lax.all_gather(moving, 'snap', axis=0, tiled=True), weigh...  13.2 us
    all_to_all x1, starting transfers between devices, on_device(): lax.all_to_all(outgoing, 'space', split_axis=1, concat_axis=1, tiled=True)  9.58 us
  transfers between devices with their start and end apart: 3, of which 3 were waited for; matrix products, arithmetic and copies ran while one was open for 1% of the time, Pallas kernels for 0%

commit v1 on v0

--- a/solution.py
+++ b/solution.py
@@ -4,6 +4,13 @@
 from jax.sharding import PartitionSpec as P
 
 PEN_LEN = 128
+
+
+def exchange_gather(x, axis, dim):
+    peers = lax.axis_size(axis)
+    pieces = jnp.stack([x for _ in range(peers)])
+    pieces = lax.all_to_all(pieces, axis, split_axis=0, concat_axis=0)
+    return jnp.concatenate(pieces, axis=dim)
 
 
 def on_device(primal, adjoint_pencils, weights, pencil_map):
@@ -28,7 +35,7 @@
         rows_here, points
     )
     product = lax.dot_general(
-        lax.all_gather(moving, "snap", axis=0, tiled=True),
+        exchange_gather(moving, "snap", 0),
         weighted,
         (((1,), (1,)), ((), ())),
         preferred_element_type=jnp.float32,

time: 309 us -> 437 us (1.41)
  blocking collectives: 0 us -> 280 us
  waiting for transfers between devices: 255 us -> 103 us
    all_to_all x0 -> x1, blocking collectives: none -> 280 us  [exchange_gather(): pieces = lax.all_to_all(pieces, axis, split_axis=0, concat_axis=0)]
    all_gather x1 -> x0, waiting for transfers between devices: 149 us -> none  [on_device(): lax.all_gather(moving, 'snap', axis=0, tiled=True)]
  transfers between devices with their start and end apart: 3 -> 2, of which waited for: 3 -> 2; matrix products, arithmetic and copies ran while one was open for 1% -> 1% of each run, Pallas kernels for 0% -> 0%
where the time goes in v1:
time: 437 us
  blocking collectives  280 us (64%)
  waiting for transfers between devices  103 us (24%)
  between operations  13.5 us (3%)
  matrix products  12.4 us (3%)
  local copies, waits for them, and re-layouts  10.2 us (2%)
  starting transfers between devices  9.62 us (2%)
  other arithmetic  8.65 us (2%)
    all_to_all x1, blocking collectives, exchange_gather(): pieces = lax.all_to_all(pieces, axis, split_axis=0, concat_axis=0)  280 us
    reduce_scatter x1, waiting for transfers between devices, on_device(): return lax.psum_scatter(product, 'space', scatter_dimension=0, tiled=True)  67.6 us
    all_to_all x1, waiting for transfers between devices, on_device(): lax.all_to_all(outgoing, 'space', split_axis=1, concat_axis=1, tiled=True)  35.2 us
    dot_general x1, matrix products, on_device(): lax.dot_general(exchange_gather(moving, 'snap', 0), weighted, (((1,), (1,...  12.4 us
    all_to_all x1, starting transfers between devices, on_device(): lax.all_to_all(outgoing, 'space', split_axis=1, concat_axis=1, tiled=True)  9.58 us
  transfers between devices with their start and end apart: 2, of which 2 were waited for; matrix products, arithmetic and copies ran while one was open for 1% of the time, Pallas kernels for 0%

profile of v1, /device:TPU:4, one launch (start us, length us, event | category | flops | bytes accessed | tf_op | source)
XLA Modules:
  0.0 437.2 jit_solution(9819858457399209294)
XLA Ops:
  6.5 0.9 reshape.40
  7.4 0.1 copy.12
  7.5 1.5 sort.34
  9.1 0.2 dynamic-slice_reduce_fusion
  9.3 0.4 copy_bitcast_fusion.1
  9.7 2.0 gather_fusion.1
  11.7 2.8 broadcast_select_fusion
  14.5 9.6 %all-to-all-start = ((bf16[64,16,6,128]{3,0,2,1:T(8,128)(2,1)}), bf16[64,16,6,128]{3,0,2,1:T(8,128)(2,1)S(1)}, u32[]{:S(2)}, u32[]{:S(2)}) async-start(bf16[64,16,6,128]{3,0,2,1:T(8,128)(2,1)} %bitcast.23), calls=%async_computation | async-start | bytes 3145728 | tf_op jit(solution)/shard_map/all_to_all | solution.py:32
  24.1 0.0 reduce-scatter.2.cloned.1.call-start
  24.1 0.1 copy.13
  24.2 0.1 reshape.61
  24.3 1.2 gather_fusion
  25.6 0.1 reshape.64
  25.6 0.1 copy.14
  25.7 0.1 copy.15
  25.8 0.1 sub.19
  25.9 2.5 sort.35
  28.5 35.2 %all-to-all-done = bf16[64,16,6,128]{3,0,2,1:T(8,128)(2,1)S(1)} async-done(((bf16[64,16,6,128]{3,0,2,1:T(8,128)(2,1)}), bf16[64,16,6,128]{3,0,2,1:T(8,128)(2,1)S(1)}, u32[]{:S(2)}, u32[]{:S(2)}) %all-to-all-start) | async-done | bytes 1572896 | tf_op jit(solution)/shard_map/all_to_all | solution.py:32
  63.7 2.0 gather_fusion.2
  65.6 1.7 copy_bitcast_fusion
  67.4 3.0 stack.3
  70.4 279.9 %all_to_all.10 = bf16[16,64,12288]{2,1,0:T(8,128)(2,1)} all-to-all(bf16[16,64,12288]{2,1,0:T(8,128)(2,1)S(1)} %stack.3), channel_id=1, replica_groups=mesh['space'=16,'snap'=16] {'snap'}, dimensions={0} | all-to-all | bytes 50331648 | tf_op jit(solution)/shard_map/all_to_all | solution.py:12
  350.3 12.4 %fusion = f32[1024,128]{1,0:T(8,128)} fusion(bf16[1024,12288]{1,0:T(8,128)(2,1)} %bitcast.21, bf16[128,12288]{1,0:T(8,128)(2,1)S(1)} %copy-done.1, f32[12288]{0:T(1024)S(1)} %copy-done.2), kind=kOutput, calls=%fused_computation.4 | convolution fusion | flops 3225944064 | bytes 28884992 | tf_op jit(solution)/shard_map/dot_general | solution.py:37
  362.7 67.6 %reduce-scatter.2.cloned.1.call-done = f32[64,128]{1,0:T(8,128)} async-done(((f32[1024,128]{1,0:T(8,128)}), f32[64,128]{1,0:T(8,128)}) %reduce-scatter.2.cloned.1.call-update) | async-done | bytes 32784 | tf_op jit(solution)/shard_map/reduce_scatter | solution.py:43
  (18 shorter events, 0.1 us)
Async XLA Ops:
  6.5 2.7 copy-start
  14.5 49.2 %all-to-all-start = ((bf16[64,16,6,128]{3,0,2,1:T(8,128)(2,1)}), bf16[64,16,6,128]{3,0,2,1:T(8,128)(2,1)S(1)}, u32[]{:S(2)}, u32[]{:S(2)}) async-start(bf16[64,16,6,128]{3,0,2,1:T(8,128)(2,1)} %bitcast.23), calls=%async_computation | async-start | bytes 3145728 | tf_op jit(solution)/shard_map/all_to_all | solution.py:32
  24.1 406.3 %reduce-scatter.2.cloned.1.call-start = ((), (), s32[]{:S(2)}) async-start(), calls=%async_computation.3 | async-start | bytes 557056 | tf_op jit(solution)/shard_map/reduce_scatter | solution.py:43
  70.3 279.9 %copy-start.1 = (bf16[128,12288]{1,0:T(8,128)(2,1)S(1)}, bf16[128,12288]{1,0:T(8,128)(2,1)}, u32[]{:S(2)}) copy-start(bf16[128,12288]{1,0:T(8,128)(2,1)} %param.6) | copy-start | bytes 9437188
  70.3 279.9 %copy-start.2 = (f32[12288]{0:T(1024)S(1)}, f32[12288]{0:T(1024)}, u32[]{:S(2)}) copy-start(f32[12288]{0:T(1024)} %param.8) | copy-start | bytes 147460
Sparse Core Ops, SparseCore 0:
  362.8 67.4 reduce-scatter.1
